TPU v7x, 32 devices: a whole 2x2x4 slice. The times are simulated.
32 devices in a mesh: dp: 8 (over z, core), tensor: 4 (over y, x).
Axes of the slice: x: 2, y: 2, z: 4, core: 2. Of those that a mesh axis runs over, the one named last changes fastest.
Arguments:
- inputs: bfloat16 [49152, 512], P(('dp', 'tensor')), may hold values from -6 to 6
- w_qkv: bfloat16 [2, 3, 512, 512], P(None, None, 'dp', 'tensor'), may hold values from -0.25 to 0.25
- w_out: bfloat16 [2, 512, 512], P(None, 'tensor', 'dp'), may hold values from -0.75 to 0.75
- w_up: bfloat16 [2, 512, 2048], P(None, 'dp', 'tensor'), may hold values from -0.25 to 0.25
- w_down: bfloat16 [2, 2048, 512], P(None, 'tensor', 'dp'), may hold values from -0.125 to 0.125
- ln_gain: float32 [2, 2, 512], replicated, may hold values from 0.5 to 1.5
- ln_bias: float32 [2, 2, 512], replicated, may hold values from -3 to 3
- bias_qv: float32 [2, 2, 512], P(None, None, 'tensor'), may hold values from -3 to 3
- bias_up: float32 [2, 2048], P(None, 'tensor'), may hold values from -3 to 3
- branch_bias: float32 [2, 2, 512], replicated, may hold values from -3 to 3
- cotangent: float32 [49152, 512], P(('dp', 'tensor')), may hold values from -6 to 6
Outputs:
- outputs: bfloat16 [49152, 512], P(('dp', 'tensor'))
- input_grad: float32 [49152, 512], P(('dp', 'tensor'))
- grad_qkv: float32 [2, 3, 512, 512], P(None, None, 'dp', 'tensor')
- grad_out: float32 [2, 512, 512], P(None, 'tensor', 'dp')
- grad_up: float32 [2, 512, 2048], P(None, 'dp', 'tensor')
- grad_down: float32 [2, 2048, 512], P(None, 'tensor', 'dp')
- grad_ln_gain: float32 [2, 2, 512], replicated
- grad_ln_bias: float32 [2, 2, 512], replicated
- grad_bias_qv: float32 [2, 2, 512], P(None, None, 'tensor')
- grad_bias_up: float32 [2, 2048], P(None, 'tensor')
- grad_branch_bias: float32 [2, 2, 512], replicated
All inputs are finite; a program needn't handle non-finite values.
Results may differ from a plain program's by a relative error of at most 0.025.
Values may be sent and summed in bfloat16 or wider, within the bound.
A program may use at most 320 MiB of HBM per device.

v0:
```python
import math
import jax
import jax.numpy as jnp
from jax import lax
from jax.sharding import PartitionSpec as P

HD = 64
SPAN = 128
LEN = 2048
LAYERS = 2
highest = lax.Precision.HIGHEST
epsilon = 1e-05
masked_score = -1e30


def normalize(rows, gain, shift):
    centre = rows - jnp.mean(rows, -1, keepdims=True)
    spread = jnp.mean(centre * centre, -1, keepdims=True)
    return centre * lax.rsqrt(spread + epsilon) * gain + shift


def gelu_exact(values):
    return jax.nn.gelu(values, approximate=False)


def to_heads(rows):
    return rows.reshape(-1, LEN // SPAN, SPAN, rows.shape[1] // HD, HD)


def score_blocks(head_queries, head_keys, key_mean):
    scale = HD ** (-0.5)
    blocks = LEN // SPAN
    direct = (
        jnp.einsum(
            "gbihe,gbjhe->gbhij", head_queries, head_keys, preferred_element_type=jnp.float32
        )
        * scale
    )
    summary = jnp.einsum(
        "gbihe,gche->gbhic", head_queries.astype(jnp.float32), key_mean, precision=highest
    ) * scale + math.log(SPAN)
    inside = lax.broadcasted_iota(jnp.int32, (SPAN, SPAN), 0) >= lax.broadcasted_iota(
        jnp.int32, (SPAN, SPAN), 1
    )
    earlier = lax.broadcasted_iota(jnp.int32, (blocks, 1, 1, blocks), 0) > lax.broadcasted_iota(
        jnp.int32, (blocks, 1, 1, blocks), 3
    )
    return (jnp.where(inside, direct, masked_score), jnp.where(earlier, summary, masked_score))


def attend(query_rows, key_rows, value_rows):
    head_queries, head_keys, head_values = (
        to_heads(query_rows),
        to_heads(key_rows),
        to_heads(value_rows),
    )
    key_mean = jnp.mean(head_keys.astype(jnp.float32), 2)
    value_mean = jnp.mean(head_values.astype(jnp.float32), 2)
    direct, summary = score_blocks(head_queries, head_keys, key_mean)
    top = jnp.maximum(jnp.max(direct, -1), jnp.max(summary, -1))[..., None]
    direct_weight = jnp.exp(direct - top)
    summary_weight = jnp.exp(summary - top)
    total = jnp.sum(direct_weight, -1, keepdims=True) + jnp.sum(summary_weight, -1, keepdims=True)
    direct_prob = direct_weight / total
    summary_prob = summary_weight / total
    mixed = jnp.einsum(
        "gbhij,gbjhe->gbihe",
        direct_prob.astype(jnp.bfloat16),
        head_values,
        preferred_element_type=jnp.float32,
    )
    mixed = mixed + jnp.einsum("gbhic,gche->gbihe", summary_prob, value_mean, precision=highest)
    log_total = (top + jnp.log(total))[..., 0]
    return (mixed.reshape(query_rows.shape), log_total)


def attend_back(query_rows, key_rows, value_rows, log_total, grad_rows):
    scale = HD ** (-0.5)
    head_queries, head_keys, head_values = (
        to_heads(query_rows),
        to_heads(key_rows),
        to_heads(value_rows),
    )
    head_grads = to_heads(grad_rows)
    key_mean = jnp.mean(head_keys.astype(jnp.float32), 2)
    value_mean = jnp.mean(head_values.astype(jnp.float32), 2)
    direct, summary = score_blocks(head_queries, head_keys, key_mean)
    direct_prob = jnp.exp(direct - log_total[..., None])
    summary_prob = jnp.exp(summary - log_total[..., None])
    grad_float = head_grads.astype(jnp.float32)
    query_float = head_queries.astype(jnp.float32)
    direct_grad = jnp.einsum(
        "gbihe,gbjhe->gbhij", head_grads, head_values, preferred_element_type=jnp.float32
    )
    summary_grad = jnp.einsum("gbihe,gche->gbhic", grad_float, value_mean, precision=highest)
    centre = jnp.sum(direct_prob * direct_grad, -1, keepdims=True) + jnp.sum(
        summary_prob * summary_grad, -1, keepdims=True
    )
    direct_score = (direct_prob * (direct_grad - centre)).astype(jnp.bfloat16)
    summary_score = summary_prob * (summary_grad - centre)
    grad_query = jnp.einsum(
        "gbhij,gbjhe->gbihe", direct_score, head_keys, preferred_element_type=jnp.float32
    )
    grad_query = (
        grad_query + jnp.einsum("gbhic,gche->gbihe", summary_score, key_mean, precision=highest)
    ) * scale
    key_block = jnp.einsum("gbhic,gbihe->gche", summary_score, query_float, precision=highest) * (
        scale / SPAN
    )
    grad_key = (
        jnp.einsum(
            "gbhij,gbihe->gbjhe", direct_score, head_queries, preferred_element_type=jnp.float32
        )
        * scale
        + key_block[:, :, None]
    )
    value_block = (
        jnp.einsum("gbhic,gbihe->gche", summary_prob, grad_float, precision=highest) / SPAN
    )
    grad_value = (
        jnp.einsum(
            "gbhij,gbihe->gbjhe",
            direct_prob.astype(jnp.bfloat16),
            head_grads,
            preferred_element_type=jnp.float32,
        )
        + value_block[:, :, None]
    )
    shape = query_rows.shape
    return (grad_query.reshape(shape), grad_key.reshape(shape), grad_value.reshape(shape))


def fetch(first, second, third, fourth):
    return (
        lax.all_gather(first, "dp", axis=2, tiled=True),
        lax.all_gather(second, "dp", axis=2, tiled=True),
        lax.all_gather(third, "dp", axis=1, tiled=True),
        lax.all_gather(fourth, "dp", axis=2, tiled=True),
    )


def return_grads(first, second, third, fourth):
    return (
        lax.psum_scatter(first.astype(jnp.bfloat16), "dp", scatter_dimension=2, tiled=True).astype(
            jnp.float32
        ),
        lax.psum_scatter(second.astype(jnp.bfloat16), "dp", scatter_dimension=2, tiled=True).astype(
            jnp.float32
        ),
        lax.psum_scatter(third.astype(jnp.bfloat16), "dp", scatter_dimension=1, tiled=True).astype(
            jnp.float32
        ),
        lax.psum_scatter(fourth.astype(jnp.bfloat16), "dp", scatter_dimension=2, tiled=True).astype(
            jnp.float32
        ),
    )


def layer_weights(w_qkv, w_out, w_up, w_down, layer):
    gathered = fetch(
        w_qkv[layer : layer + 1],
        w_out[layer : layer + 1],
        w_up[layer : layer + 1],
        w_down[layer : layer + 1],
    )
    return tuple((part[0] for part in gathered))


def spread_only(rows, project):
    return project(lax.all_gather(rows, "tensor", axis=0, tiled=True))


def fold_again(rows, grads):
    return jnp.einsum(
        "td,tc->dc",
        lax.all_gather(rows, "tensor", axis=0, tiled=True),
        grads,
        preferred_element_type=jnp.float32,
    )


def spread_grads(rows, project):
    piece = lax.all_gather(rows, "tensor", axis=0, tiled=True)
    return (piece, project(piece))


def slice_term(source, weight, form):
    return jnp.einsum(form, source, weight, preferred_element_type=jnp.float32)


def rows_sum(source, weight, form):
    return lax.psum_scatter(
        slice_term(source, weight, form).astype(jnp.bfloat16),
        "tensor",
        scatter_dimension=0,
        tiled=True,
    ).astype(jnp.float32)


def grads_sum(source, weight, form):
    return lax.psum_scatter(
        slice_term(source, weight, form).astype(jnp.bfloat16),
        "tensor",
        scatter_dimension=0,
        tiled=True,
    ).astype(jnp.float32)


def group_rows(token_att, out_whole):
    groups = lax.axis_size("tensor")
    parts = token_att.reshape(token_att.shape[0], groups, -1)
    grouped = out_whole.reshape(groups, -1, out_whole.shape[1])
    partial_value = jnp.einsum("tgc,gcd->tgd", parts, grouped, preferred_element_type=jnp.float32)
    return jnp.sum(partial_value.astype(jnp.bfloat16), 1, dtype=jnp.float32)


def group_grads(token_grads, qkv_whole):
    groups = lax.axis_size("tensor")
    parts = token_grads.reshape(token_grads.shape[0], 3, groups, -1)
    grouped = qkv_whole.reshape(3, qkv_whole.shape[1], groups, -1)
    partial_value = jnp.einsum("tsgc,sdgc->tgd", parts, grouped, preferred_element_type=jnp.float32)
    return jnp.sum(partial_value.astype(jnp.bfloat16), 1, dtype=jnp.float32)


def forward_layer(residual, matrices, gains, shifts, bias_pair, bias_hidden, branch_pair):
    w_qkv, w_out, w_up, w_down = matrices
    attn_in = normalize(residual, gains[0], shifts[0]).astype(jnp.bfloat16)

    def project_qkv(piece):
        return jnp.einsum("td,sdc->tsc", piece, w_qkv, preferred_element_type=jnp.float32)

    def project_up(piece):
        return jnp.dot(piece, w_up, preferred_element_type=jnp.float32)

    mixed_qkv = spread_only(attn_in, project_qkv)
    queries = (mixed_qkv[:, 0] + bias_pair[0]).astype(jnp.bfloat16)
    keys_now = mixed_qkv[:, 1].astype(jnp.bfloat16)
    values_now = (mixed_qkv[:, 2] + bias_pair[1]).astype(jnp.bfloat16)
    mixed, log_total = attend(queries, keys_now, values_now)
    attended = mixed.astype(jnp.bfloat16)
    qkv_whole, out_whole = (
        lax.all_gather(w_qkv, "tensor", axis=2, tiled=True),
        lax.all_gather(w_out, "tensor", axis=0, tiled=True),
    )
    token_att = lax.all_to_all(attended, "tensor", split_axis=0, concat_axis=1, tiled=True)
    attn_branch = group_rows(token_att, out_whole)
    middle = residual + attn_branch + branch_pair[0]
    mlp_in = normalize(middle, gains[1], shifts[1]).astype(jnp.bfloat16)
    raised = spread_only(mlp_in, project_up)
    hidden = raised + bias_hidden
    activated = gelu_exact(hidden).astype(jnp.bfloat16)
    result = middle + rows_sum(activated, w_down, "tc,cd->td") + branch_pair[1]
    saved = (
        residual,
        middle,
        attn_in,
        mlp_in,
        None,
        None,
        queries,
        keys_now,
        values_now,
        log_total,
        attended,
        hidden,
        activated,
        qkv_whole,
    )
    return (result, saved)


def backward_layer(grad_residual, saved, matrices, gains, shifts):
    w_qkv, w_out, w_up, w_down = matrices
    (
        residual,
        middle,
        attn_in,
        mlp_in,
        attn_rows,
        mlp_rows,
        queries,
        keys_now,
        values_now,
        log_total,
        attended,
        hidden,
        activated,
        qkv_whole,
    ) = saved
    down_bias_grad = jnp.sum(grad_residual, 0)

    def back_down(piece):
        return jnp.einsum("td,fd->tf", piece, w_down, preferred_element_type=jnp.float32)

    gathered_out, grad_act = spread_grads(grad_residual.astype(jnp.bfloat16), back_down)
    down_grad = jnp.einsum("tf,td->fd", activated, gathered_out, preferred_element_type=jnp.float32)
    grad_hidden = jax.vjp(gelu_exact, hidden)[1](grad_act)[0].astype(jnp.bfloat16)
    up_bias_grad = jnp.sum(grad_hidden, 0, dtype=jnp.float32)
    up_grad = fold_again(mlp_in, grad_hidden)
    grad_mlp_in = grads_sum(grad_hidden, w_up, "tf,df->td")
    norm_back = jax.vjp(normalize, middle, gains[1], shifts[1])[1]
    grad_norm, gain_second, shift_second = norm_back(grad_mlp_in)
    grad_middle = grad_residual + grad_norm
    attn_bias_grad = jnp.sum(grad_middle, 0)

    def back_out(piece):
        return jnp.einsum("td,cd->tc", piece, w_out, preferred_element_type=jnp.float32)

    gathered_mid, grad_attended = spread_grads(grad_middle.astype(jnp.bfloat16), back_out)
    out_grad = jnp.einsum("tc,td->cd", attended, gathered_mid, preferred_element_type=jnp.float32)
    grad_query, grad_key, grad_value = attend_back(
        queries, keys_now, values_now, log_total, grad_attended.astype(jnp.bfloat16)
    )
    grad_query = grad_query.astype(jnp.bfloat16)
    grad_key = grad_key.astype(jnp.bfloat16)
    grad_value = grad_value.astype(jnp.bfloat16)
    pair_grad = jnp.stack(
        [jnp.sum(grad_query, 0, dtype=jnp.float32), jnp.sum(grad_value, 0, dtype=jnp.float32)]
    )
    stacked = jnp.stack([grad_query, grad_key, grad_value], 1)
    flat_grad = fold_again(attn_in, stacked.reshape(stacked.shape[0], -1))
    qkv_grad = jnp.transpose(flat_grad.reshape(flat_grad.shape[0], 3, -1), (1, 0, 2))
    token_grads = lax.all_to_all(stacked, "tensor", split_axis=0, concat_axis=2, tiled=True)
    grad_attn_in = group_grads(token_grads, qkv_whole)
    first_back = jax.vjp(normalize, residual, gains[0], shifts[0])[1]
    grad_first, gain_first, shift_first = first_back(grad_attn_in)
    grad_input = grad_middle + grad_first
    matrix_part = (qkv_grad[None], out_grad[None], up_grad[None], down_grad[None])
    shared_part = (
        jnp.stack([gain_first, gain_second]),
        jnp.stack([shift_first, shift_second]),
        jnp.stack([attn_bias_grad, down_bias_grad]),
    )
    head_part = (pair_grad, up_bias_grad)
    return (grad_input, matrix_part, shared_part, head_part)


def body(
    inputs, w_qkv, w_out, w_up, w_down, ln_gain, ln_bias, bias_qv, bias_up, branch_bias, cotangent
):
    residual = inputs.astype(jnp.float32)
    saved_all = []
    for layer in range(LAYERS):
        matrices = layer_weights(w_qkv, w_out, w_up, w_down, layer)
        residual, saved = forward_layer(
            residual,
            matrices,
            ln_gain[layer],
            ln_bias[layer],
            bias_qv[layer],
            bias_up[layer],
            branch_bias[layer],
        )
        saved_all.append(saved)
    outputs = residual.astype(jnp.bfloat16)
    grad_residual = cotangent
    matrix_grads = [None] * LAYERS
    shared_grads = [None] * LAYERS
    head_grads = [None] * LAYERS
    for layer in reversed(range(LAYERS)):
        matrices = layer_weights(w_qkv, w_out, w_up, w_down, layer)
        grad_residual, matrix_part, shared_part, head_part = backward_layer(
            grad_residual, saved_all[layer], matrices, ln_gain[layer], ln_bias[layer]
        )
        matrix_grads[layer] = return_grads(
            matrix_part[0], matrix_part[1], matrix_part[2], matrix_part[3]
        )
        shared_grads[layer] = shared_part
        head_grads[layer] = head_part
    joined = [jnp.concatenate([grads[index] for grads in matrix_grads], 0) for index in range(4)]
    gain_total = jnp.stack([grads[0] for grads in shared_grads])
    shift_total = jnp.stack([grads[1] for grads in shared_grads])
    branch_total = jnp.stack([grads[2] for grads in shared_grads])
    gain_sum, shift_sum, branch_sum = lax.psum(
        (gain_total, shift_total, branch_total), ("dp", "tensor")
    )
    pair_total = jnp.stack([grads[0] for grads in head_grads])
    hidden_total = jnp.stack([grads[1] for grads in head_grads])
    pair_sum, hidden_sum = lax.psum((pair_total, hidden_total), "dp")
    return (
        outputs,
        grad_residual,
        joined[0],
        joined[1],
        joined[2],
        joined[3],
        gain_sum,
        shift_sum,
        pair_sum,
        hidden_sum,
        branch_sum,
    )


def solution(mesh):
    return jax.shard_map(
        body,
        mesh=mesh,
        in_specs=(
            P(("dp", "tensor"), None),
            P(None, None, "dp", "tensor"),
            P(None, "tensor", "dp"),
            P(None, "dp", "tensor"),
            P(None, "tensor", "dp"),
            P(),
            P(),
            P(None, None, "tensor"),
            P(None, "tensor"),
            P(),
            P(("dp", "tensor"), None),
        ),
        out_specs=(
            P(("dp", "tensor"), None),
            P(("dp", "tensor"), None),
            P(None, None, "dp", "tensor"),
            P(None, "tensor", "dp"),
            P(None, "dp", "tensor"),
            P(None, "tensor", "dp"),
            P(),
            P(),
            P(None, None, "tensor"),
            P(None, "tensor"),
            P(),
        ),
        check_vma=False,
    )
```

profile of v0, /device:TPU:12, one launch (start us, length us, event | category | flops | bytes accessed | tf_op | source)
XLA Modules:
  0.0 1674.3 jit_solution(17339127591960681586)
XLA Ops:
  31.0 55.3 %all-gather.15.cloned.1.call-done = bf16[6144,512]{1,0:T(8,128)(2,1)} async-done(((bf16[1536,512]{1,0:T(8,128)(2,1)}), bf16[6144,512]{1,0:T(8,128)(2,1)}) %all-gather.15.cloned.1.call-update) | async-done | bytes 6291472 | tf_op jit(solution)/shard_map/all_gather | solution.py:170
  178.9 15.7 all_gather.75
  194.6 16.1 all_gather.76
  210.7 36.6 %all-gather.17.cloned.1.call-done = bf16[6144,512]{1,0:T(8,128)(2,1)} async-done(((bf16[1536,512]{1,0:T(8,128)(2,1)}), bf16[6144,512]{1,0:T(8,128)(2,1)}) %all-gather.17.cloned.1.call-update) | async-done | bytes 6291472 | tf_op jit(solution)/shard_map/all_gather | solution.py:170
  247.2 33.3 %multiply_convert_fusion.1 = (bf16[6144,512]{1,0:T(8,128)(2,1)S(1)}, f32[6144,512]{1,0:T(8,128)}, f32[6144,512]{1,0:T(8,128)}) fusion(f32[512]{0:T(512)S(1)} %bitcast.514, bf16[6144,512]{1,0:T(8,128)(2,1)} %all-gather.17.cloned.1.call-done, bf16[1,512,512]{2,1,0:T(8,128)(2,1)} %all_gather.75), kind=kOutput, calls=%fused_computation.28 | convolution fusion | flops 3428843520 | bytes 38275072 | tf_op jit(solution)/shard_map/dot_general | solution.py:233
  288.7 70.2 %reduce-scatter.21.cloned.1.call-done = bf16[1536,512]{1,0:T(8,128)(2,1)} async-done(((bf16[6144,512]{1,0:T(8,128)(2,1)}), bf16[1536,512]{1,0:T(8,128)(2,1)}) %reduce-scatter.21.cloned.1.call-update) | async-done | bytes 1572880 | tf_op jit(solution)/shard_map/reduce_scatter | solution.py:192
  364.4 14.9 all_gather.78
  379.3 55.4 %all-gather.19.cloned.1.call-done = bf16[6144,512]{1,0:T(8,128)(2,1)} async-done(((bf16[1536,512]{1,0:T(8,128)(2,1)}), bf16[6144,512]{1,0:T(8,128)(2,1)}) %all-gather.19.cloned.1.call-update) | async-done | bytes 6291472 | tf_op jit(solution)/shard_map/all_gather | solution.py:170
  530.8 15.2 all_gather.82
  545.9 15.1 all_gather.83
  561.1 37.8 %all-gather.21.cloned.1.call-done = bf16[6144,512]{1,0:T(8,128)(2,1)} async-done(((bf16[1536,512]{1,0:T(8,128)(2,1)}), bf16[6144,512]{1,0:T(8,128)(2,1)}) %all-gather.21.cloned.1.call-update) | async-done | bytes 6291472 | tf_op jit(solution)/shard_map/all_gather | solution.py:170
  598.8 33.1 %multiply_convert_fusion = (bf16[6144,512]{1,0:T(8,128)(2,1)}, f32[6144,512]{1,0:T(8,128)}, f32[6144,512]{1,0:T(8,128)}) fusion(f32[512]{0:T(512)S(1)} %bitcast.517, bf16[6144,512]{1,0:T(8,128)(2,1)} %all-gather.21.cloned.1.call-done, bf16[1,512,512]{2,1,0:T(8,128)(2,1)S(1)} %all_gather.82), kind=kOutput, calls=%fused_computation.14 | convolution fusion | flops 3428843520 | bytes 38275072 | tf_op jit(solution)/shard_map/dot_general | solution.py:233
  631.9 38.8 %all-gather.23.cloned.1.call-done = bf16[6144,512]{1,0:T(8,128)(2,1)} async-done(((bf16[1536,512]{1,0:T(8,128)(2,1)}), bf16[6144,512]{1,0:T(8,128)(2,1)}) %all-gather.23.cloned.1.call-update) | async-done | bytes 6291472 | tf_op jit(solution)/shard_map/all_gather | solution.py:183
  701.7 61.4 %reduce-scatter.25.cloned.1.call-done = bf16[1536,512]{1,0:T(8,128)(2,1)} async-done(((bf16[6144,512]{1,0:T(8,128)(2,1)}), bf16[1536,512]{1,0:T(8,128)(2,1)}) %reduce-scatter.25.cloned.1.call-update) | async-done | bytes 1572880 | tf_op jit(solution)/shard_map/reduce_scatter | solution.py:201
  768.9 67.4 %reduce-scatter.23.cloned.1.call-done = bf16[1536,512]{1,0:T(8,128)(2,1)} async-done(((bf16[6144,512]{1,0:T(8,128)(2,1)}), bf16[1536,512]{1,0:T(8,128)(2,1)}) %reduce-scatter.23.cloned.1.call-update) | async-done | bytes 1572880 | tf_op jit(solution)/shard_map/reduce_scatter | solution.py:192
  844.5 70.4 %all-gather.25.cloned.1.call-done = bf16[6144,512]{1,0:T(8,128)(2,1)} async-done(((bf16[1536,512]{1,0:T(8,128)(2,1)}), bf16[6144,512]{1,0:T(8,128)(2,1)}) %all-gather.25.cloned.1.call-update) | async-done | bytes 6291472 | tf_op jit(solution)/shard_map/all_gather | solution.py:183
  992.6 68.5 %all-gather.31.cloned.1.call-done = bf16[1,3,512,512]{3,2,1,0:T(8,128)(2,1)} async-done(((bf16[1,3,512,128]{3,2,1,0:T(8,128)(2,1)}), bf16[1,3,512,512]{3,2,1,0:T(8,128)(2,1)}) %all-gather.31.cloned.1.call-update) | async-done | bytes 1572880 | tf_op jit(solution)/shard_map/all_gather | solution.py:242
  1090.3 72.9 %all-gather.27.cloned.1.call-done = bf16[6144,512]{1,0:T(8,128)(2,1)} async-done(((bf16[1536,512]{1,0:T(8,128)(2,1)}), bf16[6144,512]{1,0:T(8,128)(2,1)}) %all-gather.27.cloned.1.call-update) | async-done | bytes 6291472 | tf_op jit(solution)/shard_map/all_gather | solution.py:183
  1200.9 54.0 %reduce-scatter.27.cloned.1.call-done = bf16[1536,512]{1,0:T(8,128)(2,1)} async-done(((bf16[6144,512]{1,0:T(8,128)(2,1)}), bf16[1536,512]{1,0:T(8,128)(2,1)}) %reduce-scatter.27.cloned.1.call-update) | async-done | bytes 1572880 | tf_op jit(solution)/shard_map/reduce_scatter | solution.py:201
  1327.2 63.8 %all-gather.29.cloned.1.call-done = bf16[6144,512]{1,0:T(8,128)(2,1)} async-done(((bf16[1536,512]{1,0:T(8,128)(2,1)}), bf16[6144,512]{1,0:T(8,128)(2,1)}) %all-gather.29.cloned.1.call-update) | async-done | bytes 6291472 | tf_op jit(solution)/shard_map/all_gather | solution.py:183
  1484.2 30.2 %reduce-scatter.33.cloned.1.call-done = bf16[1,64,512]{2,1,0:T(8,128)(2,1)} async-done(((bf16[1,512,512]{2,1,0:T(8,128)(2,1)}), bf16[1,64,512]{2,1,0:T(8,128)(2,1)}) %reduce-scatter.33.cloned.1.call-update) | async-done | bytes 65552 | tf_op jit(solution)/shard_map/reduce_scatter | solution.py:150
  1546.6 29.4 %reduce-scatter.31.cloned.1.call-done = bf16[1,3,64,128]{3,2,1,0:T(8,128)(2,1)} async-done(((bf16[1,3,512,128]{3,2,1,0:T(8,128)(2,1)}), bf16[1,3,64,128]{3,2,1,0:T(8,128)(2,1)}) %reduce-scatter.31.cloned.1.call-update) | async-done | bytes 49168 | tf_op jit(solution)/shard_map/reduce_scatter | solution.py:144
  1576.0 31.2 %reduce-scatter.29.cloned.1.call-done = bf16[1,3,64,128]{3,2,1,0:T(8,128)(2,1)} async-done(((bf16[1,3,512,128]{3,2,1,0:T(8,128)(2,1)}), bf16[1,3,64,128]{3,2,1,0:T(8,128)(2,1)}) %reduce-scatter.29.cloned.1.call-update) | async-done | bytes 49168 | tf_op jit(solution)/shard_map/reduce_scatter | solution.py:144
  1622.8 44.5 %all-reduce = (f32[2,2,512]{2,1,0:T(2,128)}, f32[2,2,512]{2,1,0:T(2,128)}, f32[2,2,512]{2,1,0:T(2,128)}) all-reduce(f32[2,2,512]{2,1,0:T(2,128)S(1)} %pad_maximum_fusion, f32[2,2,512]{2,1,0:T(2,128)S(1)} %pad_maximum_fusion.1, f32[2,2,512]{2,1,0:T(2,128)S(1)} %pad_maximum_fusion.2), channel_id=1, replica_groups=mesh['dp'=8,'tensor'=4] {'dp','tensor'}, use_global_device_ids=true, to_apply=%region_52.53 | all-reduce | flops 6144 | bytes 49152 | tf_op jit(solution)/shard_map/psum | solution.py:374
  (560 shorter events, 626.7 us)
Async XLA Ops:
  7.2 79.1 %all-gather.15.cloned.1.call-start = ((), (), s32[]{:S(2)}) async-start(), calls=%async_computation.16 | async-start | bytes 7864320 | tf_op jit(solution)/shard_map/all_gather | solution.py:170
  143.5 103.8 %all-gather.17.cloned.1.call-start = ((), (), s32[]{:S(2)}) async-start(), calls=%async_computation.17 | async-start | bytes 7864320 | tf_op jit(solution)/shard_map/all_gather | solution.py:170
  176.9 182.0 %reduce-scatter.21.cloned.1.call-start = ((), (), s32[]{:S(2)}) async-start(), calls=%async_computation.18 | async-start | bytes 7864320 | tf_op jit(solution)/shard_map/reduce_scatter | solution.py:192
  288.7 146.0 %all-gather.19.cloned.1.call-start = ((), (), s32[]{:S(2)}) async-start(), calls=%async_computation.19 | async-start | bytes 7864320 | tf_op jit(solution)/shard_map/all_gather | solution.py:170
  492.5 106.3 %all-gather.21.cloned.1.call-start = ((), (), s32[]{:S(2)}) async-start(), calls=%async_computation.20 | async-start | bytes 7864320 | tf_op jit(solution)/shard_map/all_gather | solution.py:170
  527.9 142.8 %all-gather.23.cloned.1.call-start = ((), (), s32[]{:S(2)}) async-start(), calls=%async_computation.22 | async-start | bytes 7864320 | tf_op jit(solution)/shard_map/all_gather | solution.py:183
  530.7 232.4 %reduce-scatter.25.cloned.1.call-start = ((), (), s32[]{:S(2)}) async-start(), calls=%async_computation.23 | async-start | bytes 7864320 | tf_op jit(solution)/shard_map/reduce_scatter | solution.py:201
  692.9 143.4 %reduce-scatter.23.cloned.1.call-start = ((), (), s32[]{:S(2)}) async-start(), calls=%async_computation.21 | async-start | bytes 7864320 | tf_op jit(solution)/shard_map/reduce_scatter | solution.py:192
  701.3 213.7 %all-gather.25.cloned.1.call-start = ((), (), s32[]{:S(2)}) async-start(), calls=%async_computation.24 | async-start | bytes 7864320 | tf_op jit(solution)/shard_map/all_gather | solution.py:183
  986.2 88.0 %all-to-all-start.2 = ((bf16[6144,3,128]{2,1,0:T(4,128)(2,1)}), bf16[6144,3,128]{2,1,0:T(4,128)(2,1)}, u32[]{:S(2)}, u32[]{:S(2)}) async-start(bf16[6144,3,128]{2,1,0:T(4,128)(2,1)} %copy.393), calls=%async_computation.5 | async-start | bytes 12582912 | tf_op jit(solution)/shard_map/all_to_all | solution.py:323
  992.0 69.1 %all-gather.31.cloned.1.call-start = ((), (), s32[]{:S(2)}) async-start(), calls=%async_computation.32 | async-start | bytes 1966080 | tf_op jit(solution)/shard_map/all_gather | solution.py:242
  992.6 170.6 %all-gather.27.cloned.1.call-start = ((), (), s32[]{:S(2)}) async-start(), calls=%async_computation.25 | async-start | bytes 7864320 | tf_op jit(solution)/shard_map/all_gather | solution.py:183
  1090.2 164.6 %reduce-scatter.27.cloned.1.call-start = ((), (), s32[]{:S(2)}) async-start(), calls=%async_computation.26 | async-start | bytes 7864320 | tf_op jit(solution)/shard_map/reduce_scatter | solution.py:201
  1184.6 103.1 %all-gather.33.cloned.1.call-start = ((), (), s32[]{:S(2)}) async-start(), calls=%async_computation.33 | async-start | bytes 1966080 | tf_op jit(solution)/shard_map/all_gather | solution.py:242
  1185.4 131.8 %reduce-scatter.43.cloned.1.call-start = ((), (), s32[]{:S(2)}) async-start(), calls=%async_computation.37 | async-start | bytes 589824
  1200.8 190.2 %all-gather.29.cloned.1.call-start = ((), (), s32[]{:S(2)}) async-start(), calls=%async_computation.27 | async-start | bytes 7864320 | tf_op jit(solution)/shard_map/all_gather | solution.py:183
  1264.2 209.2 %reduce-scatter.39.cloned.1.call-start = ((), (), s32[]{:S(2)}) async-start(), calls=%async_computation.35 | async-start | bytes 147456
  1271.3 203.1 %reduce-scatter.41.cloned.1.call-start = ((), (), s32[]{:S(2)}) async-start(), calls=%async_computation.36 | async-start | bytes 589824
  1281.3 202.9 %reduce-scatter.35.cloned.1.call-start = ((), (), s32[]{:S(2)}) async-start(), calls=%async_computation.31 | async-start | bytes 589824 | tf_op jit(solution)/shard_map/reduce_scatter | solution.py:150
  1302.8 211.6 %reduce-scatter.33.cloned.1.call-start = ((), (), s32[]{:S(2)}) async-start(), calls=%async_computation.30 | async-start | bytes 589824 | tf_op jit(solution)/shard_map/reduce_scatter | solution.py:150
  1454.7 154.0 %all-to-all-start.3 = ((bf16[6144,3,128]{2,1,0:T(4,128)(2,1)}), bf16[6144,3,128]{2,1,0:T(4,128)(2,1)}, u32[]{:S(2)}, u32[]{:S(2)}) async-start(bf16[6144,3,128]{2,1,0:T(4,128)(2,1)} %copy.417), calls=%async_computation.7 | async-start | bytes 12582912 | tf_op jit(solution)/shard_map/all_to_all | solution.py:323
  1460.6 84.4 %reduce-scatter.37.cloned.1.call-start = ((), (), s32[]{:S(2)}) async-start(), calls=%async_computation.34 | async-start | bytes 147456
  1465.3 110.7 %reduce-scatter.31.cloned.1.call-start = ((), (), s32[]{:S(2)}) async-start(), calls=%async_computation.29 | async-start | bytes 442368 | tf_op jit(solution)/shard_map/reduce_scatter | solution.py:144
  1473.3 133.8 %reduce-scatter.29.cloned.1.call-start = ((), (), s32[]{:S(2)}) async-start(), calls=%async_computation.28 | async-start | bytes 442368 | tf_op jit(solution)/shard_map/reduce_scatter | solution.py:144
  (135 other events, 2140.6 us)
Sparse Core Ops, SparseCore 0:
  15.0 71.2 all-gather.14
  177.1 70.1 all-gather.16
  288.8 70.0 reduce-scatter.20
  364.3 70.3 all-gather.18
  528.0 70.7 all-gather.20
  600.5 70.1 all-gather.22
  693.0 70.0 reduce-scatter.24
  766.1 70.1 reduce-scatter.22
  844.6 70.3 all-gather.24
  994.3 66.7 all-gather.30
  1090.4 72.8 all-gather.26
  1184.8 70.0 reduce-scatter.26
  1256.7 30.9 all-gather.32
  1289.8 27.3 reduce-scatter.42
  1319.1 71.9 all-gather.28
  1393.8 26.6 reduce-scatter.38
  1422.6 28.9 reduce-scatter.40
  1453.8 29.1 reduce-scatter.34
  1485.3 29.0 reduce-scatter.32
  1516.5 28.3 reduce-scatter.36
  1547.2 28.7 reduce-scatter.30
  1578.4 28.7 reduce-scatter.28
where the time goes:
time: 1690 us; the launch traced here: 1670 us
  waiting for transfers between devices  890 us (53%)
  matrix products  278 us (16%)
  blocking collectives  200 us (12%)
  local copies, waits for them, and re-layouts  189 us (11%)
  other arithmetic  78.1 us (5%)
  starting transfers between devices  22.5 us (1%)
    all_gather x4, waiting for transfers between devices, spread_grads(): piece = lax.all_gather(rows, 'tensor', axis=0, tiled=True)  246 us
    all_gather x4, waiting for transfers between devices, spread_only(): return project(lax.all_gather(rows, 'tensor', axis=0, tiled=True))  185 us
    reduce_scatter x2, waiting for transfers between devices, rows_sum(): lax.psum_scatter(slice_term(source, weight, form).astype(jnp.bfloat16), '...  138 us
    reduce_scatter x2, waiting for transfers between devices, grads_sum(): lax.psum_scatter(slice_term(source, weight, form).astype(jnp.bfloat16), '...  115 us
    all_gather x2, waiting for transfers between devices, forward_layer(): lax.all_gather(w_qkv, 'tensor', axis=2, tiled=True)  74.7 us
    dot_general x2, matrix products, project_up(): return jnp.dot(piece, w_up, preferred_element_type=jnp.float32)  66.4 us
    reduce_scatter x2, waiting for transfers between devices, return_grads(): lax.psum_scatter(first.astype(jnp.bfloat16), 'dp', scatter_dimension=2, t...  60.6 us
    unnamed x296, local copies, waits for them, and re-layouts  59.3 us
  transfers between devices with their start and end apart: 26, of which 20 were waited for; matrix products, arithmetic and copies ran while one was open for 13% of the time, Pallas kernels for 0%

commit v1 on v0

--- a/solution.py
+++ b/solution.py
@@ -11,6 +11,19 @@
 highest = lax.Precision.HIGHEST
 epsilon = 1e-05
 masked_score = -1e30
+
+
+def collect(array, axis, dim):
+    ways = lax.axis_size(axis)
+    up = [(d, (d + 1) % ways) for d in range(ways)]
+    down = [(d, (d - 1) % ways) for d in range(ways)]
+    earlier, later = ([array], [array])
+    for _ in range(ways // 2):
+        earlier.append(lax.ppermute(earlier[-1], axis, up))
+    for _ in range((ways - 1) // 2):
+        later.append(lax.ppermute(later[-1], axis, down))
+    line = jnp.concatenate([*earlier[::-1], *later[1:]], axis=dim)
+    return jnp.roll(line, (lax.axis_index(axis) - ways // 2) * array.shape[dim], axis=dim)
 
 
 def normalize(rows, gain, shift):
@@ -167,7 +180,7 @@
 
 
 def spread_only(rows, project):
-    return project(lax.all_gather(rows, "tensor", axis=0, tiled=True))
+    return project(collect(rows, "tensor", 0))
 
 
 def fold_again(rows, grads):

time: 1690 us -> 2200 us (1.30)
  waiting for transfers between devices: 890 us -> 1310 us
  matrix products: 278 us -> 359 us
    ppermute x0 -> x12, waiting for transfers between devices: none -> 353 us  [the longest x8 300 us: collect(): earlier.append(lax.ppermute(earlier[-1], axis, up))]
    unnamed x26, waiting for transfers between devices: 29.9 us -> 87.7 us
    dot_general x2, matrix products: 66.4 us -> 111 us  [project_up(): return jnp.dot(piece, w_up, preferred_element_type=jnp.float32)]
    all_gather x4, waiting for transfers between devices: 246 us -> 207 us  [spread_grads(): piece = lax.all_gather(rows, 'tensor', axis=0, tiled=True)]
    dot_general x2, matrix products: 11 us -> 47.7 us  [project_qkv(): jnp.einsum('td,sdc->tsc', piece, w_qkv, preferred_element_type=jnp.float32)]
    all_gather x4, waiting for transfers between devices: 185 us -> 210 us  [fold_again(): lax.all_gather(rows, 'tensor', axis=0, tiled=True)]
    reduce_scatter x2, waiting for transfers between devices: 30.2 us -> 53.4 us  [return_grads(): lax.psum_scatter(third.astype(jnp.bfloat16), 'dp', scatter_dimension=1, t...]
    unnamed x296 -> x320, local copies, waits for them, and re-layouts: 59.3 us -> 58.5 us
  transfers between devices with their start and end apart: 26 -> 38, of which waited for: 20 -> 33; matrix products, arithmetic and copies ran while one was open for 13% -> 11% of each run, Pallas kernels for 0% -> 0%
where the time goes in v1:
time: 2200 us; the launch traced here: 2190 us
  waiting for transfers between devices  1310 us (60%)
  matrix products  359 us (16%)
  local copies, waits for them, and re-layouts  198 us (9%)
  blocking collectives  198 us (9%)
  other arithmetic  75.7 us (3%)
  starting transfers between devices  34.2 us (2%)
    ppermute x8, waiting for transfers between devices, collect(): earlier.append(lax.ppermute(earlier[-1], axis, up))  300 us
    all_gather x4, waiting for transfers between devices, fold_again(): lax.all_gather(rows, 'tensor', axis=0, tiled=True)  210 us
    all_gather x4, waiting for transfers between devices, spread_grads(): piece = lax.all_gather(rows, 'tensor', axis=0, tiled=True)  207 us
    reduce_scatter x2, waiting for transfers between devices, rows_sum(): lax.psum_scatter(slice_term(source, weight, form).astype(jnp.bfloat16), '...  138 us
    reduce_scatter x2, waiting for transfers between devices, grads_sum(): lax.psum_scatter(slice_term(source, weight, form).astype(jnp.bfloat16), '...  114 us
    dot_general x2, matrix products, project_up(): return jnp.dot(piece, w_up, preferred_element_type=jnp.float32)  111 us
    unnamed x26, waiting for transfers between devices  87.7 us
    all_gather x2, waiting for transfers between devices, forward_layer(): lax.all_gather(w_qkv, 'tensor', axis=2, tiled=True)  74.2 us
  transfers between devices with their start and end apart: 38, of which 33 were waited for; matrix products, arithmetic and copies ran while one was open for 11% of the time, Pallas kernels for 0%

profile of v1, /device:TPU:12, one launch (start us, length us, event | category | flops | bytes accessed | tf_op | source)
XLA Modules:
  0.0 2189.6 jit_solution(9094403434782645555)
XLA Ops:
  16.1 35.4 %collective-permute-done = bf16[1536,512]{1,0:T(8,128)(2,1)} collective-permute-done((bf16[1536,512]{1,0:T(8,128)(2,1)S(1)}, bf16[1536,512]{1,0:T(8,128)(2,1)}, u32[]{:S(2)}, u32[]{:S(2)}) %collective-permute-start) | collective-permute-done | bytes 1572896 | tf_op jit(solution)/shard_map/ppermute | solution.py:22
  84.2 33.5 %collective-permute-done.1 = bf16[1536,512]{1,0:T(8,128)(2,1)} collective-permute-done((bf16[1536,512]{1,0:T(8,128)(2,1)}, bf16[1536,512]{1,0:T(8,128)(2,1)}, u32[]{:S(2)}, u32[]{:S(2)}) %collective-permute-start.1) | collective-permute-done | bytes 1572896 | tf_op jit(solution)/shard_map/ppermute | solution.py:22
  234.9 35.5 %collective-permute-done.3 = bf16[1536,512]{1,0:T(8,128)(2,1)S(1)} collective-permute-done((bf16[1536,512]{1,0:T(8,128)(2,1)}, bf16[1536,512]{1,0:T(8,128)(2,1)S(1)}, u32[]{:S(2)}, u32[]{:S(2)}) %collective-permute-start.3) | collective-permute-done | bytes 1572896 | tf_op jit(solution)/shard_map/ppermute | solution.py:22
  303.3 32.5 %collective-permute-done.4 = bf16[1536,512]{1,0:T(8,128)(2,1)S(1)} collective-permute-done((bf16[1536,512]{1,0:T(8,128)(2,1)S(1)}, bf16[1536,512]{1,0:T(8,128)(2,1)S(1)}, u32[]{:S(2)}, u32[]{:S(2)}) %collective-permute-start.4) | collective-permute-done | bytes 1572896 | tf_op jit(solution)/shard_map/ppermute | solution.py:22
  335.8 59.4 %multiply_convert_fusion.1 = (bf16[6144,512]{1,0:T(8,128)(2,1)S(1)}, f32[6144,512]{1,0:T(8,128)}, f32[6144,512]{1,0:T(8,128)}) fusion(f32[512]{0:T(512)S(1)} %bitcast.512, bf16[1,512,512]{2,1,0:T(8,128)(2,1)S(1)} %all_gather.69, s32[]{:T(128)S(6)} %select_n.39, bf16[1536,512]{1,0:T(8,128)(2,1)S(1)} %collective-permute-done.4, ...), kind=kOutput, calls=%fused_computation.60 | convolution fusion | flops 3479175168 | bytes 38275076 | tf_op jit(solution)/shard_map/dot_general | solution.py:246
  403.2 70.3 %reduce-scatter.21.cloned.1.call-done = bf16[1536,512]{1,0:T(8,128)(2,1)} async-done(((bf16[6144,512]{1,0:T(8,128)(2,1)}), bf16[1536,512]{1,0:T(8,128)(2,1)}) %reduce-scatter.21.cloned.1.call-update) | async-done | bytes 1572880 | tf_op jit(solution)/shard_map/reduce_scatter | solution.py:205
  480.6 35.4 %collective-permute-done.6 = bf16[1536,512]{1,0:T(8,128)(2,1)} collective-permute-done((bf16[1536,512]{1,0:T(8,128)(2,1)S(1)}, bf16[1536,512]{1,0:T(8,128)(2,1)}, u32[]{:S(2)}, u32[]{:S(2)}) %collective-permute-start.6) | collective-permute-done | bytes 1572896 | tf_op jit(solution)/shard_map/ppermute | solution.py:22
  549.0 33.3 %collective-permute-done.7 = bf16[1536,512]{1,0:T(8,128)(2,1)} collective-permute-done((bf16[1536,512]{1,0:T(8,128)(2,1)}, bf16[1536,512]{1,0:T(8,128)(2,1)}, u32[]{:S(2)}, u32[]{:S(2)}) %collective-permute-start.7) | collective-permute-done | bytes 1572896 | tf_op jit(solution)/shard_map/ppermute | solution.py:22
  701.8 35.6 %collective-permute-done.9 = bf16[1536,512]{1,0:T(8,128)(2,1)} collective-permute-done((bf16[1536,512]{1,0:T(8,128)(2,1)}, bf16[1536,512]{1,0:T(8,128)(2,1)}, u32[]{:S(2)}, u32[]{:S(2)}) %collective-permute-start.9) | collective-permute-done | bytes 1572896 | tf_op jit(solution)/shard_map/ppermute | solution.py:22
  787.8 58.7 %collective-permute-done.10 = bf16[1536,512]{1,0:T(8,128)(2,1)} collective-permute-done((bf16[1536,512]{1,0:T(8,128)(2,1)}, bf16[1536,512]{1,0:T(8,128)(2,1)}, u32[]{:S(2)}, u32[]{:S(2)}) %collective-permute-start.10) | collective-permute-done | bytes 1572896 | tf_op jit(solution)/shard_map/ppermute | solution.py:22
  846.5 51.1 %multiply_convert_fusion = (bf16[6144,512]{1,0:T(8,128)(2,1)}, f32[6144,512]{1,0:T(8,128)}, f32[6144,512]{1,0:T(8,128)}) fusion(f32[512]{0:T(512)S(1)} %bitcast.515, bf16[1,512,512]{2,1,0:T(8,128)(2,1)S(1)} %all_gather.74, s32[]{:T(128)S(6)} %select_n.39, bf16[1536,512]{1,0:T(8,128)(2,1)} %collective-permute-done.10, ...), kind=kOutput, calls=%fused_computation.46 | convolution fusion | flops 3479175168 | bytes 38275076 | tf_op jit(solution)/shard_map/dot_general | solution.py:246
  928.4 61.4 %reduce-scatter.25.cloned.1.call-done = bf16[1536,512]{1,0:T(8,128)(2,1)} async-done(((bf16[6144,512]{1,0:T(8,128)(2,1)}), bf16[1536,512]{1,0:T(8,128)(2,1)}) %reduce-scatter.25.cloned.1.call-update) | async-done | bytes 1572880 | tf_op jit(solution)/shard_map/reduce_scatter | solution.py:214
  995.6 67.2 %reduce-scatter.23.cloned.1.call-done = bf16[1536,512]{1,0:T(8,128)(2,1)} async-done(((bf16[6144,512]{1,0:T(8,128)(2,1)}), bf16[1536,512]{1,0:T(8,128)(2,1)}) %reduce-scatter.23.cloned.1.call-update) | async-done | bytes 1572880 | tf_op jit(solution)/shard_map/reduce_scatter | solution.py:205
  1071.1 70.4 %all-gather.17.cloned.1.call-done = bf16[6144,512]{1,0:T(8,128)(2,1)} async-done(((bf16[1536,512]{1,0:T(8,128)(2,1)}), bf16[6144,512]{1,0:T(8,128)(2,1)}) %all-gather.17.cloned.1.call-update) | async-done | bytes 6291472 | tf_op jit(solution)/shard_map/all_gather | solution.py:196
  1219.3 68.5 %all-gather.31.cloned.1.call-done = bf16[1,3,512,512]{3,2,1,0:T(8,128)(2,1)} async-done(((bf16[1,3,512,128]{3,2,1,0:T(8,128)(2,1)}), bf16[1,3,512,512]{3,2,1,0:T(8,128)(2,1)}) %all-gather.31.cloned.1.call-update) | async-done | bytes 1572880 | tf_op jit(solution)/shard_map/all_gather | solution.py:255
  1317.0 72.9 %all-gather.19.cloned.1.call-done = bf16[6144,512]{1,0:T(8,128)(2,1)} async-done(((bf16[1536,512]{1,0:T(8,128)(2,1)}), bf16[6144,512]{1,0:T(8,128)(2,1)}) %all-gather.19.cloned.1.call-update) | async-done | bytes 6291472 | tf_op jit(solution)/shard_map/all_gather | solution.py:196
  1428.9 52.9 %reduce-scatter.27.cloned.1.call-done = bf16[1536,512]{1,0:T(8,128)(2,1)} async-done(((bf16[6144,512]{1,0:T(8,128)(2,1)}), bf16[1536,512]{1,0:T(8,128)(2,1)}) %reduce-scatter.27.cloned.1.call-update) | async-done | bytes 1572880 | tf_op jit(solution)/shard_map/reduce_scatter | solution.py:214
  1520.9 65.7 %all-gather.29.cloned.1.call-done = bf16[6144,512]{1,0:T(8,128)(2,1)} async-done(((bf16[1536,512]{1,0:T(8,128)(2,1)}), bf16[6144,512]{1,0:T(8,128)(2,1)}) %all-gather.29.cloned.1.call-update) | async-done | bytes 6291472 | tf_op jit(solution)/shard_map/all_gather | solution.py:189
  1617.3 72.7 %all-gather.27.cloned.1.call-done = bf16[6144,512]{1,0:T(8,128)(2,1)} async-done(((bf16[1536,512]{1,0:T(8,128)(2,1)}), bf16[6144,512]{1,0:T(8,128)(2,1)}) %all-gather.27.cloned.1.call-update) | async-done | bytes 6291472 | tf_op jit(solution)/shard_map/all_gather | solution.py:189
  1698.9 63.3 %all-gather.21.cloned.1.call-done = bf16[6144,512]{1,0:T(8,128)(2,1)} async-done(((bf16[1536,512]{1,0:T(8,128)(2,1)}), bf16[6144,512]{1,0:T(8,128)(2,1)}) %all-gather.21.cloned.1.call-update) | async-done | bytes 6291472 | tf_op jit(solution)/shard_map/all_gather | solution.py:196
  1897.0 71.8 %all-gather.23.cloned.1.call-done = bf16[6144,512]{1,0:T(8,128)(2,1)} async-done(((bf16[1536,512]{1,0:T(8,128)(2,1)}), bf16[6144,512]{1,0:T(8,128)(2,1)}) %all-gather.23.cloned.1.call-update) | async-done | bytes 6291472 | tf_op jit(solution)/shard_map/all_gather | solution.py:189
  1998.4 31.5 %reduce-scatter.33.cloned.1.call-done = bf16[1,64,512]{2,1,0:T(8,128)(2,1)} async-done(((bf16[1,512,512]{2,1,0:T(8,128)(2,1)}), bf16[1,64,512]{2,1,0:T(8,128)(2,1)}) %reduce-scatter.33.cloned.1.call-update) | async-done | bytes 65552 | tf_op jit(solution)/shard_map/reduce_scatter | solution.py:163
  2091.4 31.2 %reduce-scatter.29.cloned.1.call-done = bf16[1,3,64,128]{3,2,1,0:T(8,128)(2,1)} async-done(((bf16[1,3,512,128]{3,2,1,0:T(8,128)(2,1)}), bf16[1,3,64,128]{3,2,1,0:T(8,128)(2,1)}) %reduce-scatter.29.cloned.1.call-update) | async-done | bytes 49168 | tf_op jit(solution)/shard_map/reduce_scatter | solution.py:157
  2138.1 44.4 %all-reduce = (f32[2,2,512]{2,1,0:T(2,128)}, f32[2,2,512]{2,1,0:T(2,128)}, f32[2,2,512]{2,1,0:T(2,128)}) all-reduce(f32[2,2,512]{2,1,0:T(2,128)S(1)} %pad_maximum_fusion, f32[2,2,512]{2,1,0:T(2,128)S(1)} %pad_maximum_fusion.1, f32[2,2,512]{2,1,0:T(2,128)S(1)} %pad_maximum_fusion.2), channel_id=1, replica_groups=mesh['dp'=8,'tensor'=4] {'dp','tensor'}, use_global_device_ids=true, to_apply=%region_52.54 | all-reduce | flops 6144 | bytes 49152 | tf_op jit(solution)/shard_map/psum | solution.py:387
  (608 shorter events, 918.3 us)
Async XLA Ops:
  197.8 275.7 %reduce-scatter.21.cloned.1.call-start = ((), (), s32[]{:S(2)}) async-start(), calls=%async_computation.16 | async-start | bytes 7864320 | tf_op jit(solution)/shard_map/reduce_scatter | solution.py:205
  663.0 234.7 %all-gather.15.cloned.1.call-start = ((), (), s32[]{:S(2)}) async-start(), calls=%async_computation.18 | async-start | bytes 7864320 | tf_op jit(solution)/shard_map/all_gather | solution.py:196
  737.4 109.0 %collective-permute-start.10 = (bf16[1536,512]{1,0:T(8,128)(2,1)}, bf16[1536,512]{1,0:T(8,128)(2,1)}, u32[]{:S(2)}, u32[]{:S(2)}) collective-permute-start(bf16[1536,512]{1,0:T(8,128)(2,1)} %collective-permute-done.9), channel_id=1, source_target_pairs={{0,1},{1,2},{2,3},{3,0},{4,5},{5,6},{6,7},{7,4},{8,9},{9,10},{10,1... | collective-permute-start | bytes 4718600 | tf_op jit(solution)/shard_map/ppermute | solution.py:22
  740.1 249.7 %reduce-scatter.25.cloned.1.call-start = ((), (), s32[]{:S(2)}) async-start(), calls=%async_computation.19 | async-start | bytes 7864320 | tf_op jit(solution)/shard_map/reduce_scatter | solution.py:214
  919.7 143.2 %reduce-scatter.23.cloned.1.call-start = ((), (), s32[]{:S(2)}) async-start(), calls=%async_computation.17 | async-start | bytes 7864320 | tf_op jit(solution)/shard_map/reduce_scatter | solution.py:205
  928.3 213.2 %all-gather.17.cloned.1.call-start = ((), (), s32[]{:S(2)}) async-start(), calls=%async_computation.20 | async-start | bytes 7864320 | tf_op jit(solution)/shard_map/all_gather | solution.py:196
  1212.9 88.0 %all-to-all-start.2 = ((bf16[6144,3,128]{2,1,0:T(4,128)(2,1)}), bf16[6144,3,128]{2,1,0:T(4,128)(2,1)}, u32[]{:S(2)}, u32[]{:S(2)}) async-start(bf16[6144,3,128]{2,1,0:T(4,128)(2,1)} %copy.393), calls=%async_computation.5 | async-start | bytes 12582912 | tf_op jit(solution)/shard_map/all_to_all | solution.py:336
  1219.2 170.7 %all-gather.19.cloned.1.call-start = ((), (), s32[]{:S(2)}) async-start(), calls=%async_computation.21 | async-start | bytes 7864320 | tf_op jit(solution)/shard_map/all_gather | solution.py:196
  1317.0 164.9 %reduce-scatter.27.cloned.1.call-start = ((), (), s32[]{:S(2)}) async-start(), calls=%async_computation.22 | async-start | bytes 7864320 | tf_op jit(solution)/shard_map/reduce_scatter | solution.py:214
  1411.6 103.1 %all-gather.33.cloned.1.call-start = ((), (), s32[]{:S(2)}) async-start(), calls=%async_computation.33 | async-start | bytes 1966080 | tf_op jit(solution)/shard_map/all_gather | solution.py:255
  1412.4 174.2 %all-gather.29.cloned.1.call-start = ((), (), s32[]{:S(2)}) async-start(), calls=%async_computation.30 | async-start | bytes 7864320 | tf_op jit(solution)/shard_map/all_gather | solution.py:189
  1413.0 203.3 %reduce-scatter.43.cloned.1.call-start = ((), (), s32[]{:S(2)}) async-start(), calls=%async_computation.37 | async-start | bytes 589824
  1428.3 261.7 %all-gather.27.cloned.1.call-start = ((), (), s32[]{:S(2)}) async-start(), calls=%async_computation.28 | async-start | bytes 7864320 | tf_op jit(solution)/shard_map/all_gather | solution.py:189
  1428.9 333.4 %all-gather.21.cloned.1.call-start = ((), (), s32[]{:S(2)}) async-start(), calls=%async_computation.23 | async-start | bytes 7864320 | tf_op jit(solution)/shard_map/all_gather | solution.py:196
  1491.2 345.3 %all-gather.25.cloned.1.call-start = ((), (), s32[]{:S(2)}) async-start(), calls=%async_computation.26 | async-start | bytes 7864320 | tf_op jit(solution)/shard_map/all_gather | solution.py:189
  1491.8 372.0 %reduce-scatter.39.cloned.1.call-start = ((), (), s32[]{:S(2)}) async-start(), calls=%async_computation.35 | async-start | bytes 147456
  1498.3 396.7 %reduce-scatter.41.cloned.1.call-start = ((), (), s32[]{:S(2)}) async-start(), calls=%async_computation.36 | async-start | bytes 589824
  1508.2 460.6 %all-gather.23.cloned.1.call-start = ((), (), s32[]{:S(2)}) async-start(), calls=%async_computation.24 | async-start | bytes 7864320 | tf_op jit(solution)/shard_map/all_gather | solution.py:189
  1508.8 489.6 %reduce-scatter.35.cloned.1.call-start = ((), (), s32[]{:S(2)}) async-start(), calls=%async_computation.31 | async-start | bytes 589824 | tf_op jit(solution)/shard_map/reduce_scatter | solution.py:163
  1595.4 434.4 %reduce-scatter.33.cloned.1.call-start = ((), (), s32[]{:S(2)}) async-start(), calls=%async_computation.29 | async-start | bytes 589824 | tf_op jit(solution)/shard_map/reduce_scatter | solution.py:163
  1825.8 298.3 %all-to-all-start.3 = ((bf16[6144,3,128]{2,1,0:T(4,128)(2,1)}), bf16[6144,3,128]{2,1,0:T(4,128)(2,1)}, u32[]{:S(2)}, u32[]{:S(2)}) async-start(bf16[6144,3,128]{2,1,0:T(4,128)(2,1)} %copy.417), calls=%async_computation.7 | async-start | bytes 12582912 | tf_op jit(solution)/shard_map/all_to_all | solution.py:336
  1831.8 228.6 %reduce-scatter.37.cloned.1.call-start = ((), (), s32[]{:S(2)}) async-start(), calls=%async_computation.34 | async-start | bytes 147456
  1836.4 254.9 %reduce-scatter.31.cloned.1.call-start = ((), (), s32[]{:S(2)}) async-start(), calls=%async_computation.27 | async-start | bytes 442368 | tf_op jit(solution)/shard_map/reduce_scatter | solution.py:157
  1844.4 278.1 %reduce-scatter.29.cloned.1.call-start = ((), (), s32[]{:S(2)}) async-start(), calls=%async_computation.25 | async-start | bytes 442368 | tf_op jit(solution)/shard_map/reduce_scatter | solution.py:157
  (159 other events, 4679.4 us)
Sparse Core Ops, SparseCore 0:
  403.3 70.1 reduce-scatter.20
  740.2 113.4 all-gather.14
  919.8 69.9 reduce-scatter.24
  992.6 70.2 reduce-scatter.22
  1071.2 70.2 all-gather.16
  1221.0 66.7 all-gather.30
  1317.1 72.8 all-gather.18
  1411.8 70.0 reduce-scatter.26
  1483.7 30.9 all-gather.32
  1516.4 70.1 all-gather.28
  1588.9 27.3 reduce-scatter.42
  1618.1 71.8 all-gather.26
  1692.0 70.1 all-gather.20
  1764.1 70.3 all-gather.24
  1837.2 26.5 reduce-scatter.38
  1865.9 28.9 reduce-scatter.40
  1896.8 71.9 all-gather.22
  1971.0 27.3 reduce-scatter.34
  2000.6 29.2 reduce-scatter.32
  2032.1 28.2 reduce-scatter.36
  2062.6 28.7 reduce-scatter.30
  2093.7 28.7 reduce-scatter.28
